TPU v7x, 256 devices: a whole 4x4x8 slice. The times are simulated.
256 devices in a mesh: seq: 32 (over x, z), head: 8 (over y, core).
Axes of the slice: x: 4, y: 4, z: 8, core: 2. Of those that a mesh axis runs over, the one named last changes fastest.
Arguments:
- queries: bfloat16 [4096, 8192], P('seq', 'head'), may hold values from -250 to 250
- key_vectors: bfloat16 [4096, 1024], P('seq', 'head'), may hold values from -250 to 250
- value_vectors: bfloat16 [4096, 1024], P('seq', 'head'), may hold values from -20 to 20
- positions: int32 [4096], P('seq'), may hold values from 0 to 2047, as said below
- query_map: float32 [64, 128, 128], P('head'), may hold values from -0.5 to 0.5
- key_map: float32 [8, 128, 128], P('head'), may hold values from -0.5 to 0.5
Outputs:
- grad_queries: float32 [4096, 8192], P('seq', 'head')
- grad_keys: float32 [4096, 1024], P('seq', 'head')
- grad_values: float32 [4096, 1024], P('seq', 'head')
- query_map_grad: float32 [64, 128, 128], P('head')
- key_map_grad: float32 [8, 128, 128], P('head')
Inputs may be any that keep to these rules, and one draw needn't show every extreme that they name: positions[0] is 0, and each later position is either 0 (a document begins) or one more than the position before it; the slab holds at most 4 documents, and one of them is exactly 2048 tokens long.
All inputs are finite; a program needn't handle non-finite values.
Results may differ from a plain program's by a relative error of at most 0.0025.
Values may be sent and summed in bfloat16 or wider, within the bound.
No kernel may reach another device: no remote copies, remote signals or barrier semaphores. Data moves between devices by JAX's collectives and lax.ppermute only.
A program may use at most 64 MiB of HBM per device.

v0:
```python
import math
import jax
import jax.numpy as jnp
from jax import lax
from jax.sharding import PartitionSpec as P

HIGHEST = lax.Precision.HIGHEST
NEGATIVE = -1e30
epsilon = 1e-06


def entering(value, axis, join, neutral, backward):
    count, mine = (lax.axis_size(axis), lax.axis_index(axis))
    pieces = jax.tree.map(lambda part: lax.all_gather(part, axis), value)
    if backward:
        pieces = jax.tree.map(lambda part: part[::-1], pieces)
        mine = count - 1 - mine
    running = jax.tree.map(
        lambda part, zero: jnp.full_like(part, 0) + jnp.asarray(zero, part.dtype), value, neutral
    )

    def lap(position, running):
        longer = join(running, jax.tree.map(lambda part: part[position], pieces))
        return jax.tree.map(lambda new, old: jnp.where(position < mine, new, old), longer, running)

    return lax.fori_loop(0, count - 1, lap, running)


def feature_map(logits):
    return jnp.concatenate(
        [jax.nn.softmax(logits, axis=-1), jax.nn.softmax(-logits, axis=-1)], axis=-1
    )


def feature_back(phi, grad_phi, half_width):
    upper = phi[..., :half_width]
    lower = phi[..., half_width:]
    grad_up = grad_phi[..., :half_width]
    grad_low = grad_phi[..., half_width:]
    upper_part = upper * (grad_up - jnp.sum(upper * grad_up, axis=-1, keepdims=True))
    lower_part = lower * (grad_low - jnp.sum(lower * grad_low, axis=-1, keepdims=True))
    return upper_part - lower_part


def chain_states(earlier, later):
    carried = 1.0 - later[2]
    return (
        later[0] + carried * earlier[0],
        later[1] + carried * earlier[1],
        jnp.maximum(earlier[2], later[2]),
    )


def on_device(queries, key_vectors, value_vectors, positions, query_map, key_map):
    tok_rows = queries.shape[0]
    n_group = query_map.shape[0]
    head_dim = key_vectors.shape[1]
    half_width = query_map.shape[2]
    feat_width = 2 * half_width
    my_index = lax.axis_index("seq")
    row_base = my_index * tok_rows
    row_index = row_base + jnp.arange(tok_rows, dtype=jnp.int32)
    starts = row_index - positions
    last_start = starts[-1]
    q_heads = queries.reshape(tok_rows, n_group, head_dim)
    scaling = 1.0 / math.sqrt(head_dim)
    key_float = key_vectors.astype(jnp.float32)
    value_float = value_vectors.astype(jnp.float32)
    key_logits = jnp.dot(key_float, key_map[0], precision=HIGHEST)
    key_phi = feature_map(key_logits)
    initial = (
        jnp.full((n_group, tok_rows), NEGATIVE, jnp.float32),
        jnp.zeros((n_group, tok_rows), jnp.float32),
        jnp.zeros((n_group, tok_rows, head_dim), jnp.float32),
        jnp.zeros((feat_width, head_dim), jnp.float32),
        jnp.zeros((feat_width,), jnp.float32),
    )
    key_block = lax.all_gather(key_vectors, "seq", axis=0, tiled=True)
    value_block = lax.all_gather(value_vectors, "seq", axis=0, tiled=True)
    block_len = key_block.shape[0]
    key_index = jnp.arange(block_len, dtype=jnp.int32)
    visible = (key_index[None, :] <= row_index[:, None]) & (key_index[None, :] >= starts[:, None])

    def update(current):
        run_max, row_sum, summed, state_sum, norm_sums = current
        scores = (
            jnp.einsum("tgd,nd->gtn", q_heads, key_block, preferred_element_type=jnp.float32)
            * scaling
        )
        scores = jnp.where(visible[None], scores, NEGATIVE)
        new_max = jnp.maximum(run_max, jnp.max(scores, axis=-1))
        weights = jnp.where(visible[None], jnp.exp(scores - new_max[..., None]), 0.0)
        row_sum = jnp.sum(weights, axis=-1)
        summed = jnp.einsum(
            "gtn,nd->gtd",
            weights.astype(jnp.bfloat16),
            value_block,
            preferred_element_type=jnp.float32,
        )
        return (new_max, row_sum, summed, state_sum, norm_sums)

    run_max, row_sum, summed, state_sum, norm_sums = lax.cond(
        jnp.any(visible), update, lambda current: current, initial
    )
    held_teacher = jnp.transpose(summed / row_sum[..., None], (1, 0, 2))
    query_float = q_heads.astype(jnp.float32)
    query_logits = jnp.einsum("tgd,gdf->tgf", query_float, query_map, precision=HIGHEST)
    query_phi = feature_map(query_logits)
    visible_rows = (
        (row_index[None, :] <= row_index[:, None]) & (row_index[None, :] >= starts[:, None])
    ).astype(jnp.float32)
    crossing = (starts < row_base).astype(jnp.float32)
    keeping = (starts == last_start).astype(jnp.float32)
    fresh_doc = (last_start >= row_base).astype(jnp.float32).reshape(1)
    kept_phi = key_phi * keeping[:, None]
    state_local = jnp.dot(kept_phi.T, value_float, precision=HIGHEST)
    norms_local = jnp.sum(kept_phi, axis=0)
    state_in, norms_in, unused = entering(
        (state_local, norms_local, fresh_doc),
        "seq",
        chain_states,
        (jnp.zeros_like(state_local), jnp.zeros_like(norms_local), jnp.zeros((1,), jnp.float32)),
        False,
    )
    inner = jnp.einsum("tgf,jf->gtj", query_phi, key_phi, precision=HIGHEST) * visible_rows[None]
    numer = jnp.einsum("gtj,jd->tgd", inner, value_float, precision=HIGHEST)
    numer = numer + crossing[:, None, None] * jnp.einsum(
        "tgf,fd->tgd", query_phi, state_in, precision=HIGHEST
    )
    denom = jnp.sum(inner, axis=-1).T + crossing[:, None] * jnp.einsum(
        "tgf,f->tg", query_phi, norms_in, precision=HIGHEST
    )
    outputs = numer / denom[..., None]
    error = outputs - held_teacher
    grad_numer = error / denom[..., None]
    grad_denom = -jnp.sum(error * outputs, axis=-1) / denom
    mixing = (
        jnp.einsum("tgd,jd->gtj", grad_numer, value_float, precision=HIGHEST)
        + grad_denom.T[:, :, None]
    ) * visible_rows[None]
    grad_qphi = jnp.einsum("gtj,jf->tgf", mixing, key_phi, precision=HIGHEST)
    grad_qphi = grad_qphi + crossing[:, None, None] * (
        jnp.einsum("tgd,fd->tgf", grad_numer, state_in, precision=HIGHEST)
        + grad_denom[..., None] * norms_in
    )
    crossing_phi = query_phi * crossing[:, None, None]
    back_local = jnp.einsum("tgf,tgd->fd", crossing_phi, grad_numer, precision=HIGHEST)
    back_norms = jnp.einsum("tgf,tg->f", crossing_phi, grad_denom, precision=HIGHEST)
    back_in, back_norms_in, unused_flag = entering(
        (back_local, back_norms, fresh_doc),
        "seq",
        chain_states,
        (jnp.zeros_like(back_local), jnp.zeros_like(back_norms), jnp.zeros((1,), jnp.float32)),
        True,
    )
    grad_kphi = jnp.einsum("gtj,tgf->jf", mixing, query_phi, precision=HIGHEST)
    grad_kphi = grad_kphi + keeping[:, None] * (
        jnp.dot(value_float, back_in.T, precision=HIGHEST) + back_norms_in[None, :]
    )
    grad_values = jnp.einsum("gtj,tgd->jd", inner, grad_numer, precision=HIGHEST)
    grad_values = grad_values + keeping[:, None] * jnp.dot(key_phi, back_in, precision=HIGHEST)
    query_dlogit = feature_back(query_phi, grad_qphi, half_width)
    key_dlogit = feature_back(key_phi, grad_kphi, half_width)
    grad_queries = jnp.einsum("tgf,gdf->tgd", query_dlogit, query_map, precision=HIGHEST).reshape(
        tok_rows, n_group * head_dim
    )
    grad_keys = jnp.dot(key_dlogit, key_map[0].T, precision=HIGHEST)
    local_qmap = jnp.einsum("tgd,tgf->gdf", query_float, query_dlogit, precision=HIGHEST)
    local_kmap = jnp.dot(key_float.T, key_dlogit, precision=HIGHEST)[None]
    clip_limit = 0.25 * math.sqrt((n_group + 1) * lax.axis_size("head") * head_dim * half_width)
    summed_qmap, summed_kmap = lax.psum((local_qmap, local_kmap), "seq")
    squared = lax.psum(
        jnp.sum(summed_qmap * summed_qmap) + jnp.sum(summed_kmap * summed_kmap), "head"
    )
    factor = jnp.minimum(1.0, clip_limit / (jnp.sqrt(squared) + epsilon))
    query_map_grad = factor * summed_qmap
    key_map_grad = factor * summed_kmap
    return (grad_queries, grad_keys, grad_values, query_map_grad, key_map_grad)


def solution(mesh):
    placed = (
        P("seq", "head"),
        P("seq", "head"),
        P("seq", "head"),
        P("seq"),
        P("head", None, None),
        P("head", None, None),
    )
    return jax.shard_map(
        on_device,
        mesh=mesh,
        in_specs=placed,
        out_specs=(
            P("seq", "head"),
            P("seq", "head"),
            P("seq", "head"),
            P("head", None, None),
            P("head", None, None),
        ),
        check_vma=False,
    )
```

profile of v0, /device:TPU:1, one launch (start us, length us, event | category | flops | bytes accessed | tf_op | source)
XLA Modules:
  0.0 715.1 jit_solution(13117342215060472636)
XLA Ops:
  11.8 1.6 fusion.41
  14.3 39.5 %all-gather.4 = f32[32,1,256]{2,1,0:T(1,128)S(1)} all-gather(f32[1,1,256]{2,1,0:T(1,128)S(1)} %bitcast.184), channel_id=3, replica_groups=mesh['seq'=32,'head'=8] {'seq'}, dimensions={0}, use_global_device_ids=true | all-gather | bytes 33792 | tf_op jit(solution)/shard_map/all_gather | solution.py:14
  53.8 1.8 copy.60
  59.4 57.9 %all-reduce = f32[32]{0:T(128)S(1)} all-reduce(f32[32]{0:T(128)S(1)} %dynamic-update-slice), channel_id=1, replica_groups=mesh['seq'=32,'head'=8] {'seq'}, use_global_device_ids=true, to_apply=%add | all-reduce | flops 32 | bytes 256
  120.7 2.0 convolution_bitcast_fusion.3
  122.7 39.8 %all-gather.13.cloned.1.call-done = bf16[4096,128]{1,0:T(8,128)(2,1)} async-done(((bf16[128,128]{1,0:T(8,128)(2,1)}), bf16[4096,128]{1,0:T(8,128)(2,1)}) %all-gather.13.cloned.1.call-update) | async-done | bytes 1048592 | tf_op jit(solution)/shard_map/all_gather | solution.py:79
  162.5 12.8 %conditional.1 = (f32[8,128]{1,0:T(8,128)S(1)}, f32[8,128,128]{1,2,0:T(8,128)}) conditional(s32[]{:T(128)} %convert_element_type.26, () %tuple.45, (pred[128,4096]{0,1:T(8,128)(4,1)S(1)}, bf16[4096,128]{1,0:T(8,128)(2,1)}, bf16[128,8,128]{0,2,1:T(8,128)(2,1)}, bf16[4096,128]{1,0:T(8,128)(2,1)}) %tuple.46), branch_computations={%region_13.14_spmd, %region_14.17_spmd} | conditional | flops 2202008576 | bytes 59007020 | solution.py:102
  162.5 3.8 fusion
  166.4 4.8 fusion.3
  171.2 4.0 fusion.2
  175.4 70.9 %all-gather.15.cloned.1.call-done = f32[8192,128]{1,0:T(8,128)} async-done(((f32[256,128]{1,0:T(8,128)}), f32[8192,128]{1,0:T(8,128)}) %all-gather.15.cloned.1.call-update) | async-done | bytes 4194320 | tf_op jit(solution)/shard_map/all_gather | solution.py:14
  246.3 90.0 %while.32 = (s32[]{:T(128)}, f32[256,128]{1,0:T(8,128)S(1)}, f32[256]{0:T(256)S(1)}, s32[]{:T(128)}, f32[32,256,128]{2,1,0:T(8,128)}, /*index=5*/f32[32,1]{0,1:T...) while((s32[]{:T(128)}, f32[256,128]{1,0:T(8,128)S(1)}, f32[256]{0:T(256)S(1)}, s32[]{:T(128)}, ...), condition=%wide.region_10.11_spmd.clone, body=%wide.region_9.10_spmd.clone.sunk | while | flops 132101 | bytes 398487 | solution.py:26
  247.6 1.6 fusion.106
  250.5 1.6 fusion.106
  253.4 1.6 fusion.106
  256.3 1.6 fusion.106
  259.2 1.6 fusion.106
  262.1 1.6 fusion.106
  265.0 1.6 fusion.106
  267.9 1.6 fusion.106
  270.8 1.6 fusion.106
  273.7 1.6 fusion.106
  276.6 1.6 fusion.106
  279.5 1.6 fusion.106
  282.4 1.6 fusion.106
  285.3 1.6 fusion.106
  288.2 1.6 fusion.106
  291.1 1.6 fusion.106
  294.0 1.6 fusion.106
  296.9 1.6 fusion.106
  299.8 1.6 fusion.106
  302.7 1.6 fusion.106
  305.6 1.6 fusion.106
  308.5 1.6 fusion.106
  311.4 1.6 fusion.106
  314.3 1.6 fusion.106
  317.2 1.6 fusion.106
  320.1 1.6 fusion.106
  323.1 1.6 fusion.106
  326.0 1.6 fusion.106
  328.9 1.6 fusion.106
  331.8 1.6 fusion.106
  334.7 1.6 fusion.106
  337.0 2.1 multiply_reduce_fusion.3
  339.0 1.7 convolution_bitcast_fusion.6
  341.8 32.8 %all-gather.5 = f32[32,1,256]{2,1,0:T(1,128)S(1)} all-gather(f32[1,1,256]{2,1,0:T(1,128)S(1)} %convolution_bitcast_fusion.10), channel_id=5, replica_groups=mesh['seq'=32,'head'=8] {'seq'}, dimensions={0}, use_global_device_ids=true | all-gather | bytes 33792 | tf_op jit(solution)/shard_map/all_gather | solution.py:14
  375.7 1.6 convolution_bitcast_fusion.7
  379.7 2.4 convolution_bitcast_fusion.1
  382.1 37.8 %all-gather.17.cloned.1.call-done = f32[8192,128]{1,0:T(8,128)} async-done(((f32[256,128]{1,0:T(8,128)}), f32[8192,128]{1,0:T(8,128)}) %all-gather.17.cloned.1.call-update) | async-done | bytes 4194320 | tf_op jit(solution)/shard_map/all_gather | solution.py:14
  419.9 4.6 rev.9
  424.5 109.9 %while.33 = (s32[]{:T(128)}, f32[256,128]{1,0:T(8,128)S(1)}, f32[256]{0:T(256)S(1)}, s32[]{:T(128)}, f32[32,256,128]{2,1,0:T(8,128)}, /*index=5*/f32[32,1]{0,1:T(1,128)S(1)}, f32[32,256]{1,0:T(8,128)}, s32[]{:T(128)}, s32[]{:T(128)}) while((s32[]{:T(128)}, f32[256,128]{1,0:T(8,128)S(1)}, f32[256]{0:T(256)S(1)}, s32[]{:T(128)}, ...), condition=%wide.region_21.22_spmd.clone, body=%wide.region_20.21_spmd.clone.sunk | while | flops 132101 | bytes 398487 | solution.py:26
  429.9 1.6 fusion.108
  437.0 1.6 fusion.108
  444.1 1.6 fusion.108
  451.2 1.6 fusion.108
  458.3 1.6 fusion.108
  465.4 1.6 fusion.108
  483.1 1.6 fusion.108
  490.2 1.6 fusion.108
  497.3 1.6 fusion.108
  540.4 139.9 %all-reduce.4.cloned.1.call-done = (f32[8,128,128]{1,2,0:T(8,128)}, f32[1,128,128]{1,2,0:T(8,128)}) async-done(((f32[8,128,128]{1,2,0:T(8,128)}, f32[1,128,128]{1,2,0:T(8,128)}), (f32[8,128,128]{1,2,0:T(8,128)}, f32[1,128,128]{1,2,0:T(8,128)})) %all-reduce.4.cloned.1.call-update) | async-done | bytes 589840 | tf_op jit(solution)/shard_map/psum | solution.py:171
  681.7 1.8 multiply_reduce_fusion
  684.8 1.8 fusion.44
  686.6 17.6 %psum.23 = f32[]{:T(128)} all-reduce(f32[]{:T(128)S(6)} %add.151), channel_id=1, replica_groups=mesh['seq'=32,'head'=8] {'head'}, use_global_device_ids=true, to_apply=%region_28.29 | all-reduce | flops 1 | bytes 8 | tf_op jit(solution)/shard_map/psum | solution.py:172
  (275 shorter events, 161.0 us)
Async XLA Ops:
  7.2 110.2 %copy-start = (f32[8,128,128]{2,1,0:T(8,128)S(1)}, f32[8,128,128]{2,1,0:T(8,128)}, u32[]{:S(2)}) copy-start(f32[8,128,128]{2,1,0:T(8,128)} %param.16) | copy-start | bytes 1572868
  7.2 115.5 %all-gather.11.cloned.1.call-start = ((), (), s32[]{:S(2)}) async-start(), calls=%async_computation | async-start | bytes 1081344 | tf_op jit(solution)/shard_map/all_gather | solution.py:78
  7.9 154.6 %all-gather.13.cloned.1.call-start = ((), (), s32[]{:S(2)}) async-start(), calls=%async_computation.1 | async-start | bytes 1081344 | tf_op jit(solution)/shard_map/all_gather | solution.py:79
  8.7 237.7 %all-gather.15.cloned.1.call-start = ((), (), s32[]{:S(2)}) async-start(), calls=%async_computation.2 | async-start | bytes 4325376 | tf_op jit(solution)/shard_map/all_gather | solution.py:14
  13.5 406.4 %all-gather.17.cloned.1.call-start = ((), (), s32[]{:S(2)}) async-start(), calls=%async_computation.3 | async-start | bytes 4325376 | tf_op jit(solution)/shard_map/all_gather | solution.py:14
  162.5 212.7 %copy-start.1 = (bf16[128,128]{1,0:T(8,128)(2,1)S(1)}, bf16[128,128]{1,0:T(8,128)(2,1)}, u32[]{:S(2)}) copy-start(bf16[128,128]{1,0:T(8,128)(2,1)} %param.14) | copy-start | bytes 98308
  162.5 3.8 copy-start.2
  340.7 339.6 %all-reduce.4.cloned.1.call-start = ((), (), s32[]{:S(2)}) async-start(), calls=%async_computation.4 | async-start | bytes 1179648 | tf_op jit(solution)/shard_map/psum | solution.py:171
Sparse Core Ops, SparseCore 0:
  10.6 75.4 all-gather.10
  88.7 73.7 all-gather.12
  165.1 81.1 all-gather.14
  340.8 79.0 all-gather.16
  537.3 142.9 all-reduce.3
where the time goes:
time: 720 us; the launch traced here: 715 us
  waiting for transfers between devices  290 us (40%)
  other arithmetic  190 us (26%)
  blocking collectives  148 us (21%)
  local copies, waits for them, and re-layouts  34.3 us (5%)
  matrix products  34.1 us (5%)
  between operations  17.4 us (2%)
    psum x1, waiting for transfers between devices, on_device(): summed_qmap, summed_kmap = lax.psum((local_qmap, local_kmap), 'seq')  140 us
    select_n x124, other arithmetic, lap(): jnp.where(position < mine, new, old)  140 us
    all_gather x2, waiting for transfers between devices, entering(): pieces = jax.tree.map(lambda part: lax.all_gather(part, axis), value)  109 us
    all_gather x2, blocking collectives, entering(): pieces = jax.tree.map(lambda part: lax.all_gather(part, axis), value)  72.3 us
    unnamed x1, blocking collectives  57.9 us
    all_gather x1, waiting for transfers between devices, on_device(): value_block = lax.all_gather(value_vectors, 'seq', axis=0, tiled=True)  39.8 us
    sub x62, other arithmetic, chain_states(): carried = 1.0 - later[2]  36.6 us
    dynamic_slice x62, local copies, waits for them, and re-layouts, lap(): longer = join(running, jax.tree.map(lambda part: part[position], pieces))  21.9 us
  transfers between devices with their start and end apart: 5, of which 4 were waited for; matrix products, arithmetic and copies ran while one was open for 6% of the time, Pallas kernels for 0%

commit v1 on v0

--- a/solution.py
+++ b/solution.py
@@ -76,7 +76,9 @@
         jnp.zeros((feat_width,), jnp.float32),
     )
     key_block = lax.all_gather(key_vectors, "seq", axis=0, tiled=True)
-    value_block = lax.all_gather(value_vectors, "seq", axis=0, tiled=True)
+    value_block = jnp.concatenate(
+        lax.all_to_all(jnp.stack([value_vectors] * lax.axis_size("seq")), "seq", 0, 0), axis=0
+    )
     block_len = key_block.shape[0]
     key_index = jnp.arange(block_len, dtype=jnp.int32)
     visible = (key_index[None, :] <= row_index[:, None]) & (key_index[None, :] >= starts[:, None])

time: 720 us -> 649 us (0.901)
  waiting for transfers between devices: 290 us -> 195 us
  starting transfers between devices: 0.2 us -> 12.2 us
  blocking collectives: 148 us -> 156 us
    all_gather x2, waiting for transfers between devices: 109 us -> 55 us  [entering(): pieces = jax.tree.map(lambda part: lax.all_gather(part, axis), value)]
    all_gather x1 -> x0, waiting for transfers between devices: 39.8 us -> none  [on_device(): value_block = lax.all_gather(value_vectors, 'seq', axis=0, tiled=True)]
    all_to_all x0 -> x1, starting transfers between devices: none -> 12 us  [on_device(): lax.all_to_all(jnp.stack([value_vectors] * lax.axis_size('seq')), 'seq',...]
    all_gather x2, blocking collectives: 72.3 us -> 80.3 us  [entering(): pieces = jax.tree.map(lambda part: lax.all_gather(part, axis), value)]
  transfers between devices with their start and end apart: 5 -> 5, of which waited for: 4 -> 3; matrix products, arithmetic and copies ran while one was open for 6% -> 7% of each run, Pallas kernels for 0% -> 0%
where the time goes in v1:
time: 649 us; the launch traced here: 644 us
  waiting for transfers between devices  195 us (30%)
  other arithmetic  190 us (29%)
  blocking collectives  156 us (24%)
  local copies, waits for them, and re-layouts  36.8 us (6%)
  matrix products  35.2 us (5%)
  between operations  17.4 us (3%)
  starting transfers between devices  12.2 us (2%)
    select_n x124, other arithmetic, lap(): jnp.where(position < mine, new, old)  140 us
    psum x1, waiting for transfers between devices, on_device(): summed_qmap, summed_kmap = lax.psum((local_qmap, local_kmap), 'seq')  140 us
    all_gather x2, blocking collectives, entering(): pieces = jax.tree.map(lambda part: lax.all_gather(part, axis), value)  80.3 us
    unnamed x1, blocking collectives  58.5 us
    all_gather x2, waiting for transfers between devices, entering(): pieces = jax.tree.map(lambda part: lax.all_gather(part, axis), value)  55 us
    sub x62, other arithmetic, chain_states(): carried = 1.0 - later[2]  36.6 us
    dynamic_slice x62, local copies, waits for them, and re-layouts, lap(): longer = join(running, jax.tree.map(lambda part: part[position], pieces))  22.3 us
    psum x1, blocking collectives, on_device(): lax.psum(jnp.sum(summed_qmap * summed_qmap) + jnp.sum(summed_kmap * summe...  17.6 us
  transfers between devices with their start and end apart: 5, of which 3 were waited for; matrix products, arithmetic and copies ran while one was open for 7% of the time, Pallas kernels for 0%

profile of v1, /device:TPU:1, one launch (start us, length us, event | category | flops | bytes accessed | tf_op | source)
XLA Modules:
  0.0 644.3 jit_solution(7642527102291334190)
XLA Ops:
  11.1 1.6 fusion.40
  12.7 2.0 stack.2
  14.7 12.0 %all-to-all-start = ((bf16[32,128,128]{2,1,0:T(8,128)(2,1)}), bf16[32,128,128]{2,1,0:T(8,128)(2,1)}, u32[]{:S(2)}, u32[]{:S(2)}) async-start(bf16[32,128,128]{2,1,0:T(8,128)(2,1)} %stack.2), calls=%async_computation | async-start | bytes 2097152 | tf_op jit(solution)/shard_map/all_to_all | solution.py:80
  27.4 1.8 copy.60
  31.2 48.5 %all-gather.4 = f32[32,1,256]{2,1,0:T(1,128)S(1)} all-gather(f32[1,1,256]{2,1,0:T(1,128)S(1)} %bitcast.185), channel_id=3, replica_groups=mesh['seq'=32,'head'=8] {'seq'}, dimensions={0}, use_global_device_ids=true | all-gather | bytes 33792 | tf_op jit(solution)/shard_map/all_gather | solution.py:14
  81.7 58.5 %all-reduce = f32[32]{0:T(128)S(1)} all-reduce(f32[32]{0:T(128)S(1)} %dynamic-update-slice), channel_id=1, replica_groups=mesh['seq'=32,'head'=8] {'seq'}, use_global_device_ids=true, to_apply=%add | all-reduce | flops 32 | bytes 256
  143.6 2.0 convolution_bitcast_fusion.3
  145.6 13.8 %conditional.1 = (f32[8,128]{1,0:T(8,128)S(1)}, f32[8,128,128]{1,2,0:T(8,128)}) conditional(s32[]{:T(128)} %convert_element_type.26, () %tuple.45, (pred[128,4096]{0,1:T(8,128)(4,1)S(1)}, bf16[4096,128]{1,0:T(8,128)(2,1)}, bf16[128,8,128]{0,2,1:T(8,128)(2,1)}, bf16[32,128,128]{2,1,0:T(8,128)(2,1)}) %tuple.46), branch_computations={%region_13.14_spmd, %region_14.17_spmd} | conditional | flops 2202008576 | bytes 54812688 | solution.py:104
  145.6 3.8 fusion
  149.4 4.0 fusion.2
  153.4 6.0 fusion.3
  159.4 13.3 %all-gather.12.cloned.1.call-done = f32[8192,128]{1,0:T(8,128)} async-done(((f32[256,128]{1,0:T(8,128)}), f32[8192,128]{1,0:T(8,128)}) %all-gather.12.cloned.1.call-update) | async-done | bytes 4194320 | tf_op jit(solution)/shard_map/all_gather | solution.py:14
  172.7 90.2 %while.32 = (s32[]{:T(128)}, f32[256,128]{1,0:T(8,128)S(1)}, f32[256]{0:T(256)S(1)}, s32[]{:T(128)}, f32[32,256,128]{2,1,0:T(8,128)}, /*index=5*/f32[32,1]{0,1:T...) while((s32[]{:T(128)}, f32[256,128]{1,0:T(8,128)S(1)}, f32[256]{0:T(256)S(1)}, s32[]{:T(128)}, ...), condition=%wide.region_10.11_spmd.clone, body=%wide.region_9.10_spmd.clone.sunk | while | flops 132101 | bytes 398487 | solution.py:26
  173.3 1.6 fusion.106
  176.2 1.6 fusion.106
  179.1 1.6 fusion.106
  182.0 1.6 fusion.106
  184.9 1.6 fusion.106
  187.8 1.6 fusion.106
  190.8 1.6 fusion.106
  193.7 1.6 fusion.106
  196.6 1.6 fusion.106
  199.5 1.6 fusion.106
  202.4 1.6 fusion.106
  205.3 1.6 fusion.106
  208.2 1.6 fusion.106
  211.1 1.6 fusion.106
  214.0 1.6 fusion.106
  216.9 1.6 fusion.106
  219.8 1.6 fusion.106
  222.8 1.6 fusion.106
  225.7 1.6 fusion.106
  228.6 1.6 fusion.106
  231.5 1.6 fusion.106
  234.4 1.6 fusion.106
  237.3 1.6 fusion.106
  240.2 1.6 fusion.106
  243.1 1.6 fusion.106
  246.0 1.6 fusion.106
  248.9 1.6 fusion.106
  251.8 1.6 fusion.106
  254.8 1.6 fusion.106
  257.7 1.6 fusion.106
  260.6 1.6 fusion.106
  263.5 2.1 multiply_reduce_fusion.3
  265.6 1.6 convolution_bitcast_fusion.6
  268.4 31.8 %all-gather.5 = f32[32,1,256]{2,1,0:T(1,128)S(1)} all-gather(f32[1,1,256]{2,1,0:T(1,128)S(1)} %convolution_bitcast_fusion.10), channel_id=5, replica_groups=mesh['seq'=32,'head'=8] {'seq'}, dimensions={0}, use_global_device_ids=true | all-gather | bytes 33792 | tf_op jit(solution)/shard_map/all_gather | solution.py:14
  301.2 1.6 convolution_bitcast_fusion.7
  305.2 2.4 convolution_bitcast_fusion.1
  307.6 41.7 %all-gather.14.cloned.1.call-done = f32[8192,128]{1,0:T(8,128)} async-done(((f32[256,128]{1,0:T(8,128)}), f32[8192,128]{1,0:T(8,128)}) %all-gather.14.cloned.1.call-update) | async-done | bytes 4194320 | tf_op jit(solution)/shard_map/all_gather | solution.py:14
  349.3 4.6 rev.9
  353.9 109.8 %while.33 = (s32[]{:T(128)}, f32[256,128]{1,0:T(8,128)S(1)}, f32[256]{0:T(256)S(1)}, s32[]{:T(128)}, f32[32,256,128]{2,1,0:T(8,128)}, /*index=5*/f32[32,1]{0,1:T(1,128)S(1)}, f32[32,256]{1,0:T(8,128)}, s32[]{:T(128)}, s32[]{:T(128)}) while((s32[]{:T(128)}, f32[256,128]{1,0:T(8,128)S(1)}, f32[256]{0:T(256)S(1)}, s32[]{:T(128)}, ...), condition=%wide.region_21.22_spmd.clone, body=%wide.region_20.21_spmd.clone.sunk | while | flops 132101 | bytes 398487 | solution.py:26
  354.5 1.6 fusion.108
  358.0 1.6 fusion.108
  361.5 1.6 fusion.108
  368.6 1.6 fusion.108
  372.2 1.6 fusion.108
  375.7 1.6 fusion.108
  379.3 1.6 fusion.108
  386.3 1.6 fusion.108
  469.7 139.8 %all-reduce.4.cloned.1.call-done = (f32[8,128,128]{1,2,0:T(8,128)}, f32[1,128,128]{1,2,0:T(8,128)}) async-done(((f32[8,128,128]{1,2,0:T(8,128)}, f32[1,128,128]{1,2,0:T(8,128)}), (f32[8,128,128]{1,2,0:T(8,128)}, f32[1,128,128]{1,2,0:T(8,128)})) %all-reduce.4.cloned.1.call-update) | async-done | bytes 589840 | tf_op jit(solution)/shard_map/psum | solution.py:173
  609.5 1.8 multiply_reduce_fusion
  614.0 1.8 fusion.43
  615.8 17.6 %psum.23 = f32[]{:T(128)} all-reduce(f32[]{:T(128)S(6)} %add.151), channel_id=1, replica_groups=mesh['seq'=32,'head'=8] {'head'}, use_global_device_ids=true, to_apply=%region_28.29 | all-reduce | flops 1 | bytes 8 | tf_op jit(solution)/shard_map/psum | solution.py:174
  (273 shorter events, 162.3 us)
Async XLA Ops:
  7.2 133.1 %copy-start = (f32[8,128,128]{2,1,0:T(8,128)S(1)}, f32[8,128,128]{2,1,0:T(8,128)}, u32[]{:S(2)}) copy-start(f32[8,128,128]{2,1,0:T(8,128)} %param.16) | copy-start | bytes 1572868
  7.2 138.4 %all-gather.10.cloned.1.call-start = ((), (), s32[]{:S(2)}) async-start(), calls=%async_computation.1 | async-start | bytes 1081344 | tf_op jit(solution)/shard_map/all_gather | solution.py:78
  7.9 164.8 %all-gather.12.cloned.1.call-start = ((), (), s32[]{:S(2)}) async-start(), calls=%async_computation.2 | async-start | bytes 4325376 | tf_op jit(solution)/shard_map/all_gather | solution.py:14
  14.7 130.9 %all-to-all-start = ((bf16[32,128,128]{2,1,0:T(8,128)(2,1)}), bf16[32,128,128]{2,1,0:T(8,128)(2,1)}, u32[]{:S(2)}, u32[]{:S(2)}) async-start(bf16[32,128,128]{2,1,0:T(8,128)(2,1)} %stack.2), calls=%async_computation | async-start | bytes 2097152 | tf_op jit(solution)/shard_map/all_to_all | solution.py:80
  26.7 322.6 %all-gather.14.cloned.1.call-start = ((), (), s32[]{:S(2)}) async-start(), calls=%async_computation.3 | async-start | bytes 4325376 | tf_op jit(solution)/shard_map/all_gather | solution.py:14
  145.6 155.2 %copy-start.1 = (bf16[128,128]{1,0:T(8,128)(2,1)S(1)}, bf16[128,128]{1,0:T(8,128)(2,1)}, u32[]{:S(2)}) copy-start(bf16[128,128]{1,0:T(8,128)(2,1)} %param.14) | copy-start | bytes 98308
  267.3 342.2 %all-reduce.4.cloned.1.call-start = ((), (), s32[]{:S(2)}) async-start(), calls=%async_computation.4 | async-start | bytes 1179648 | tf_op jit(solution)/shard_map/psum | solution.py:173
Sparse Core Ops, SparseCore 0:
  10.6 78.2 all-gather.9
  91.5 81.1 all-gather.11
  267.4 81.8 all-gather.13
  466.6 142.8 all-reduce.3
